TPU v7x, 32 devices: a whole 2x2x4 slice. The times are simulated.
32 devices in a mesh: lat: 4 (over z), lon: 8 (over y, x, core).
Axes of the slice: x: 2, y: 2, z: 4, core: 2. Of those that a mesh axis runs over, the one named last changes fastest.
Arguments:
- control: float32 [16, 137, 32, 1024], P('lon', None, 'lat'), may hold values from -6 to 6
- ensemble: bfloat16 [16, 137, 32, 1024], P(None, None, 'lat', 'lon'), may hold values from -2.5 to 2.5
- vertical_root: bfloat16 [137, 137], replicated, may hold values from -0.5 to 0.5
- sector_band: bfloat16 [3, 128, 1024], P(None, None, 'lon'), may hold values from -0.3125 to 0.3125
- latitude_taps: float32 [9, 1024], P(None, 'lon'), may hold values from -2 to 2
- innovation: float32 [137, 32, 1024], P(None, 'lat', 'lon'), may hold values from -6 to 6
- inverse_error: float32 [137, 32, 1024], P(None, 'lat', 'lon'), may hold values from 0.5 to 2
Outputs:
- gradient: float32 [16, 137, 32, 1024], P('lon', None, 'lat')
- departure: float32 [137, 32, 1024], P(None, 'lat', 'lon')
All inputs are finite; a program needn't handle non-finite values.
Results may differ from a plain program's by a relative error of at most 0.007.
Values may be sent and summed in bfloat16 or wider, within the bound.
A program may use at most 128 MiB of HBM per device.

v0:
```python
import jax
import jax.numpy as jnp
from jax import lax
from jax.sharding import PartitionSpec as P


def with_halo(block, sides, width):
    for axis, dim in sides:
        count = lax.axis_size(axis)
        forward = [(i, i + 1) for i in range(count - 1)]
        backward = [(target, source) for source, target in forward]
        low = lax.ppermute(
            lax.slice_in_dim(block, block.shape[dim] - width, None, axis=dim), axis, forward
        )
        high = lax.ppermute(lax.slice_in_dim(block, 0, width, axis=dim), axis, backward)
        block = jnp.concatenate([low, block, high], axis=dim)
    return block


def vertical_apply(vertical_root, fields):
    members, levels = (fields.shape[0], fields.shape[1])
    mixed = jnp.einsum(
        "lm,kmn->kln",
        vertical_root,
        fields.reshape(members, levels, -1),
        preferred_element_type=jnp.float32,
    )
    return mixed.astype(jnp.bfloat16).reshape(fields.shape)


def vertical_adjoint(vertical_root, fields):
    members, levels = (fields.shape[0], fields.shape[1])
    mixed = jnp.einsum(
        "lm,kln->kmn",
        vertical_root,
        fields.reshape(members, levels, -1),
        preferred_element_type=jnp.float32,
    )
    return mixed.astype(jnp.bfloat16).reshape(fields.shape)


def shards(control, ensemble, vertical_root, sector_band, latitude_taps, innovation, inverse_error):
    half = latitude_taps.shape[0] // 2
    width = sector_band.shape[1]
    coarse = control.astype(jnp.bfloat16)
    count = coarse.shape[3] // width
    gathered = lax.all_gather(sector_band, "lon", axis=2, tiled=True)
    band_blocks = (
        gathered.reshape(3, width, count, width)
        .transpose(2, 0, 1, 3)
        .reshape(count, 3 * width, width)
    )
    mixed = vertical_apply(vertical_root, coarse)
    blocks = mixed.reshape(-1, count, width)
    stacked = jnp.concatenate(
        [jnp.roll(blocks, 1, axis=1), blocks, jnp.roll(blocks, -1, axis=1)], axis=2
    )
    spread_members = jnp.einsum(
        "rbk,bkj->rbj", stacked, band_blocks, preferred_element_type=jnp.float32
    )
    spread_members = spread_members.astype(jnp.bfloat16).reshape(coarse.shape)
    spread = lax.all_to_all(spread_members, "lon", split_axis=3, concat_axis=0, tiled=True)
    height = spread.shape[2]
    widened_rows = with_halo(spread, (("lat", 2),), half)
    stencil = jnp.zeros(spread.shape, jnp.float32)
    for offset in range(-half, half + 1):
        stencil = stencil + latitude_taps[offset + half] * widened_rows[
            :, :, half + offset : half + offset + height, :
        ].astype(jnp.float32)
    increment = jnp.sum(ensemble.astype(jnp.float32) * stencil, axis=0)
    departure = inverse_error * (increment - innovation)
    pulled = (ensemble.astype(jnp.float32) * departure[None]).astype(jnp.bfloat16)
    widened_back = with_halo(pulled, (("lat", 2),), half)
    spread_back = jnp.zeros(pulled.shape, jnp.float32)
    for offset in range(-half, half + 1):
        spread_back = spread_back + latitude_taps[offset + half] * widened_back[
            :, :, half - offset : half - offset + height, :
        ].astype(jnp.float32)
    spread_back = spread_back.astype(jnp.bfloat16)
    member_back = lax.all_to_all(spread_back, "lon", split_axis=0, concat_axis=3, tiled=True)
    blocks_back = member_back.reshape(-1, count, width)
    terms = jnp.einsum("rbj,bkj->rbk", blocks_back, band_blocks, preferred_element_type=jnp.float32)
    terms = lax.optimization_barrier(terms.astype(jnp.bfloat16)).astype(jnp.float32)
    summed = (
        terms[..., width : 2 * width]
        + jnp.roll(terms[..., 2 * width :], 1, axis=1)
        + jnp.roll(terms[..., :width], -1, axis=1)
    )
    summed = summed.astype(jnp.bfloat16).reshape(coarse.shape)
    returned = vertical_adjoint(vertical_root, summed)
    gradient = control + returned.astype(jnp.float32)
    return (gradient, departure)


def solution(mesh):
    placed = (
        P("lon", None, "lat", None),
        P(None, None, "lat", "lon"),
        P(),
        P(None, None, "lon"),
        P(None, "lon"),
        P(None, "lat", "lon"),
        P(None, "lat", "lon"),
    )
    return jax.shard_map(
        shards,
        mesh=mesh,
        in_specs=placed,
        out_specs=(P("lon", None, "lat", None), P(None, "lat", "lon")),
        check_vma=False,
    )
```

profile of v0, /device:TPU:19, one launch (start us, length us, event | category | flops | bytes accessed | tf_op | source)
XLA Modules:
  0.0 481.7 jit_solution(504471686312627424)
XLA Ops:
  0.6 6.4 %convert_element_type.105 = bf16[2,137,8,1024]{3,2,1,0:T(8,128)(2,1)} convert(f32[2,137,8,1024]{3,2,1,0:T(8,128)} %param.7) | non-fusion elementwise | flops 2244608 | bytes 13467648 | tf_op jit(solution)/shard_map/convert_element_type | solution.py:45
  7.0 5.1 %reshape.33 = bf16[2,137,8192]{2,1,0:T(8,128)(2,1)} reshape(bf16[2,137,8,1024]{3,2,1,0:T(8,128)(2,1)} %convert_element_type.105) | data formatting | bytes 8978432 | tf_op jit(solution)/shard_map/reshape | solution.py:25
  12.1 5.9 %fusion.12 = bf16[2,137,8192]{2,1,0:T(8,128)(2,1)} fusion(bf16[2,137,8192]{2,1,0:T(8,128)(2,1)} %reshape.33, bf16[137,137]{1,0:T(8,128)(2,1)S(1)} %copy-done), kind=kOutput, calls=%fused_computation.41 | convolution fusion | flops 617267200 | bytes 9015970 | tf_op jit(solution)/shard_map/lm,kmn->kln/dot_general | solution.py:22
  18.0 5.1 %reshape_reshape.6 = bf16[2192,8,128]{2,1,0:T(8,128)(2,1)} reshape(bf16[2,137,8192]{2,1,0:T(8,128)(2,1)} %fusion.12) | data formatting | bytes 8978432 | tf_op jit(solution)/shard_map/reshape;reshape | solution.py:54
  23.1 2.9 copy.47
  27.0 11.1 %all_gather.3 = bf16[3,128,1024]{2,1,0:T(8,128)(2,1)S(1)} all-gather(bf16[3,128,128]{2,1,0:T(8,128)(2,1)S(1)} %copy-done.4), channel_id=1, replica_groups=mesh['lat'=4,'lon'=8] {'lon'}, dimensions={2}, use_global_device_ids=true | all-gather | bytes 884736 | tf_op jit(solution)/shard_map/all_gather | solution.py:47
  38.4 5.7 %fusion.20 = bf16[2192,8,128]{2,0,1:T(8,128)(2,1)S(1)} fusion(bf16[8,384,128]{2,1,0:T(8,128)(2,1)S(1)} %bitcast.65, bf16[2192,1,128]{2,0,1:T(8,128)(2,1)S(1)} %get-tuple-element.11, bf16[2192,7,128]{2,0,1:T(8,128)(2,1)S(1)} %get-tuple-element.13, bf16[2192,8,128]{2,0,1:T(8,128)(2,1)S(1)} %copy.47, bf16[2192,7,128]{2,0,1:T(8,128)(2,1)S(1)} %get-tuple-element.12, ...), kind=kOutput, calls=%fused_computation.49 | convolution fusion | flops 1793441792 | bytes 18743296 | tf_op jit(solution)/shard_map/rbk,bkj->rbj/dot_general | solution.py:58
  44.1 10.4 %copy.53 = bf16[2192,8,128]{2,1,0:T(8,128)(2,1)} copy(bf16[2192,8,128]{2,0,1:T(8,128)(2,1)S(1)} %fusion.20) | data formatting | bytes 8978432 | tf_op jit(solution)/shard_map/convert_element_type | solution.py:61
  54.5 8.0 %reshape.36 = bf16[2,137,8,1024]{3,2,1,0:T(8,128)(2,1)} reshape(bf16[2192,8,128]{2,1,0:T(8,128)(2,1)} %copy.53) | data formatting | bytes 8978432 | tf_op jit(solution)/shard_map/reshape | solution.py:61
  62.6 13.1 %copy.54 = bf16[2,137,8,1024]{1,2,0,3:T(8,128)(2,1)} copy(bf16[2,137,8,1024]{3,2,1,0:T(8,128)(2,1)} %reshape.36) | data formatting | bytes 8978432 | tf_op jit(solution)/shard_map/reshape | solution.py:61
  75.7 98.3 %all_to_all.33 = bf16[2,137,8,1024]{1,2,0,3:T(8,128)(2,1)} all-to-all(bf16[2,137,8,1024]{1,2,0,3:T(8,128)(2,1)} %copy.54), channel_id=1, replica_groups=mesh['lat'=4,'lon'=8] {'lon'}, dimensions={3} | all-to-all | bytes 8978432 | tf_op jit(solution)/shard_map/all_to_all | solution.py:62
  174.0 12.9 %copy.56 = bf16[8,2,137,8,128]{4,3,2,1,0:T(8,128)(2,1)} copy(bf16[8,2,137,8,128]{2,3,1,4,0:T(8,128)(2,1)} %bitcast.61) | data formatting | bytes 8978432 | tf_op jit(solution)/shard_map/all_to_all | solution.py:62
  186.9 5.5 %fusion.41 = (bf16[16,137,4,128]{3,2,1,0:T(4,128)(2,1)S(1)}, bf16[16,137,4,128]{3,2,1,0:T(4,128)(2,1)S(1)}) fusion(bf16[16,137,8,128]{3,2,1,0:T(8,128)(2,1)} %bitcast.57), kind=kLoop, calls=%fused_computation.83 | loop fusion | bytes 8978432 | tf_op jit(solution)/shard_map/slice | solution.py:13
  192.4 3.5 collective-permute-start
  195.9 2.1 collective-permute-start.1
  198.0 46.3 %collective-permute-done = bf16[16,137,4,128]{3,2,1,0:T(4,128)(2,1)S(1)} collective-permute-done((bf16[16,137,4,128]{3,2,1,0:T(4,128)(2,1)S(1)}, bf16[16,137,4,128]{3,2,1,0:T(4,128)(2,1)S(1)}, u32[]{:S(2)}, u32[]{:S(2)}) %collective-permute-start) | collective-permute-done | bytes 2244640 | tf_op jit(solution)/shard_map/ppermute | solution.py:12
  244.3 2.9 collective-permute-done.1
  247.2 20.3 %fusion.13 = f32[137,8,128]{2,1,0:T(8,128)S(1)} fusion(bf16[16,137,8,128]{3,2,1,0:T(8,128)(2,1)} %param.8, bf16[16,137,8,128]{3,2,1,0:T(8,128)(2,1)S(1)} %bitcast.60, bf16[16,137,4,128]{3,2,1,0:T(4,128)(2,1)S(1)} %collective-permute-done.1, bf16[16,137,4,128]{3,2,1,0:T(4,128)(2,1)S(1)} %collective-permute-done, f32[128]{0:T(128)S(1)} %get-tuple-element.21, ...), kind=kLoop, calls=%fused_computation.42 | loop fusion | flops 118823936 | bytes 14033408 | tf_op jit(solution)/shard_map/reduce_sum | solution.py:70
  272.2 3.3 collective-permute-start.3
  275.6 45.0 %collective-permute-done.2 = bf16[16,137,4,128]{3,2,1,0:T(4,128)(2,1)S(1)} collective-permute-done((bf16[16,137,4,128]{3,2,1,0:T(4,128)(2,1)S(1)}, bf16[16,137,4,128]{3,2,1,0:T(4,128)(2,1)S(1)}, u32[]{:S(2)}, u32[]{:S(2)}) %collective-permute-start.2) | collective-permute-done | bytes 2244640 | tf_op jit(solution)/shard_map/ppermute | solution.py:15
  322.3 18.0 %add_convert_fusion = bf16[16,137,8,128]{3,2,1,0:T(8,128)(2,1)S(1)} fusion(bf16[16,137,8,128]{3,2,1,0:T(8,128)(2,1)S(1)} %fusion.14, bf16[16,137,4,128]{3,2,1,0:T(4,128)(2,1)S(1)} %collective-permute-done.3, bf16[16,137,4,128]{3,2,1,0:T(4,128)(2,1)S(1)} %collective-permute-done.2, f32[128]{0:T(128)S(1)} %get-tuple-element.21, f32[128]{0:T(128)S(1)} %get-tuple-element.22, ...), kind=kLoop, calls=%fused_computation.47 | loop fusion | flops 114475008 | bytes 13472256 | tf_op jit(solution)/shard_map/convert_element_type | solution.py:79
  340.3 56.5 %all_to_all.34 = bf16[16,137,8,128]{3,2,1,0:T(8,128)(2,1)} all-to-all(bf16[16,137,8,128]{3,2,1,0:T(8,128)(2,1)S(1)} %add_convert_fusion), channel_id=1, replica_groups=mesh['lat'=4,'lon'=8] {'lon'}, dimensions={0} | all-to-all | bytes 8978432 | tf_op jit(solution)/shard_map/all_to_all | solution.py:80
  396.8 12.0 %convert_bitcast_fusion = bf16[2192,8,384]{2,0,1:T(8,128)(2,1)} fusion(bf16[2192,8,128]{2,0,1:T(8,128)(2,1)} %bitcast.64, bf16[8,384,128]{2,1,0:T(8,128)(2,1)S(1)} %bitcast.66), kind=kOutput, calls=%fused_computation.22 | convolution fusion | flops 1730592768 | bytes 18743296 | tf_op jit(solution)/shard_map/rbj,bkj->rbk/dot_general | solution.py:82
  408.8 2.8 fusion.39
  411.6 10.0 %fusion.38 = (f32[2192,7,128]{2,0,1:T(8,128)}, f32[2192,7,128]{2,0,1:T(8,128)}) fusion(bf16[2192,8,384]{2,0,1:T(8,128)(2,1)} %convert_bitcast_fusion), kind=kLoop, calls=%fused_computation.80 | loop fusion | bytes 31424512 | tf_op jit(solution)/shard_map/jit(_roll_static)/slice | solution.py:87
  421.5 6.8 %convert_element_type.132 = f32[2192,8,384]{2,0,1:T(8,128)S(1)} convert(bf16[2192,8,384]{2,0,1:T(8,128)(2,1)} %convert_bitcast_fusion) | non-fusion elementwise | flops 6733824 | bytes 40402944 | tf_op jit(solution)/shard_map/convert_element_type | solution.py:83
  428.3 7.1 %fusion.16 = bf16[2192,8,128]{2,0,1:T(8,128)(2,1)S(1)} fusion(f32[2192,8,384]{2,0,1:T(8,128)S(1)} %convert_element_type.132, f32[2192,7,128]{2,0,1:T(8,128)} %get-tuple-element.3, f32[2192,1,128]{2,0,1:T(8,128)} %get-tuple-element.5, f32[2192,1,128]{2,0,1:T(8,128)} %get-tuple-element.4, f32[2192,7,128]{2,0,1:T(8,128)} %get-tuple-element.2), kind=kLoop, calls=%fused_computation.46 | loop fusion | flops 11223040 | bytes 31424512 | tf_op jit(solution)/shard_map/convert_element_type | solution.py:89
  435.4 10.4 %copy.57 = bf16[2192,8,128]{2,1,0:T(8,128)(2,1)} copy(bf16[2192,8,128]{2,0,1:T(8,128)(2,1)S(1)} %fusion.16) | data formatting | bytes 8978432 | tf_op jit(solution)/shard_map/convert_element_type | solution.py:89
  445.9 5.0 %reshape_reshape.7 = bf16[2,137,8192]{2,1,0:T(8,128)(2,1)} reshape(bf16[2192,8,128]{2,1,0:T(8,128)(2,1)} %copy.57) | data formatting | bytes 8978432 | tf_op jit(solution)/shard_map/reshape;reshape | solution.py:36
  450.8 7.5 %fusion.11 = f32[2,137,8192]{2,1,0:T(8,128)} fusion(bf16[2,137,8192]{2,1,0:T(8,128)(2,1)} %reshape_reshape.7, bf16[137,137]{1,0:T(8,128)(2,1)S(1)} %copy-done), kind=kOutput, calls=%fused_computation.40 | convolution fusion | flops 619511808 | bytes 13505186 | tf_op jit(solution)/shard_map/lm,kln->kmn/dot_general | solution.py:33
  458.3 10.5 %reshape.38 = f32[2,137,8,1024]{3,2,1,0:T(8,128)} reshape(f32[2,137,8192]{2,1,0:T(8,128)} %fusion.11) | data formatting | bytes 17956864 | tf_op jit(solution)/shard_map/convert_element_type | solution.py:91
  468.8 12.9 %add.75 = f32[2,137,8,1024]{3,2,1,0:T(8,128)} add(f32[2,137,8,1024]{3,2,1,0:T(8,128)} %param.7, f32[2,137,8,1024]{3,2,1,0:T(8,128)} %reshape.38) | non-fusion elementwise | flops 2244608 | bytes 26935296 | tf_op jit(solution)/shard_map/add | solution.py:91
  (31 shorter events, 7.7 us)
Async XLA Ops:
  0.6 11.5 %copy-start = (bf16[137,137]{1,0:T(8,128)(2,1)S(1)}, bf16[137,137]{1,0:T(8,128)(2,1)}, u32[]{:S(2)}) copy-start(bf16[137,137]{1,0:T(8,128)(2,1)} %param.9) | copy-start | bytes 112618
  25.9 1.1 copy-start.4
  174.0 24.0 %copy-start.5 = (f32[9,128]{1,0:T(8,128)S(1)}, f32[9,128]{1,0:T(8,128)}, u32[]{:S(2)}) copy-start(f32[9,128]{1,0:T(8,128)} %param.11) | copy-start | bytes 13828
  186.9 60.4 %slice-start = ((s8[4489216]{0:T(1024)(128)(4,1)}), s8[4194304]{0:T(1024)(128)(4,1)S(1)}, s32[]{:S(2)}) async-start(s8[4489216]{0:T(1024)(128)(4,1)} %bitcast.58), calls=%async_computation.2 | async-start | bytes 8388608
  186.9 60.4 %slice-start.1 = ((s8[4489216]{0:T(1024)(128)(4,1)}), s8[294912]{0:T(1024)(128)(4,1)S(1)}, s32[]{:S(2)}) async-start(s8[4489216]{0:T(1024)(128)(4,1)} %bitcast.58), calls=%async_computation.3 | async-start | bytes 589824
  192.4 75.2 %copy-start.2 = (f32[137,8,128]{2,1,0:T(8,128)S(1)}, f32[137,8,128]{2,1,0:T(8,128)}, u32[]{:S(2)}) copy-start(f32[137,8,128]{2,1,0:T(8,128)} %param.13) | copy-start | bytes 1683460
  192.4 75.2 %copy-start.3 = (f32[137,8,128]{2,1,0:T(8,128)S(1)}, f32[137,8,128]{2,1,0:T(8,128)}, u32[]{:S(2)}) copy-start(f32[137,8,128]{2,1,0:T(8,128)} %param.12) | copy-start | bytes 1683460
  192.4 75.3 %slice-start.2 = ((s8[4489216]{0:T(1024)(128)(4,1)}), s8[4194304]{0:T(1024)(128)(4,1)S(1)}, s32[]{:S(2)}) async-start(s8[4489216]{0:T(1024)(128)(4,1)} %bitcast.62), calls=%async_computation.4 | async-start | bytes 8388608
  192.4 51.9 %collective-permute-start = (bf16[16,137,4,128]{3,2,1,0:T(4,128)(2,1)S(1)}, bf16[16,137,4,128]{3,2,1,0:T(4,128)(2,1)S(1)}, u32[]{:S(2)}, u32[]{:S(2)}) collective-permute-start(bf16[16,137,4,128]{3,2,1,0:T(4,128)(2,1)S(1)} %get-tuple-element.8), channel_id=1, source_target_pairs={{0,8},{8,16},{16,24},{1,9},{9,17},{17,25},{2,10},{10,18},{18,26},{... | collective-permute-start | bytes 6733832 | tf_op jit(solution)/shard_map/ppermute | solution.py:12
  195.9 51.3 %collective-permute-start.1 = (bf16[16,137,4,128]{3,2,1,0:T(4,128)(2,1)S(1)}, bf16[16,137,4,128]{3,2,1,0:T(4,128)(2,1)S(1)}, u32[]{:S(2)}, u32[]{:S(2)}) collective-permute-start(bf16[16,137,4,128]{3,2,1,0:T(4,128)(2,1)S(1)} %get-tuple-element.9), channel_id=1, source_target_pairs={{8,0},{16,8},{24,16},{9,1},{17,9},{25,17},{10,2},{18,10},{26,18},{... | collective-permute-start | bytes 6733832 | tf_op jit(solution)/shard_map/ppermute | solution.py:15
  247.2 20.5 %slice-start.3 = ((s8[4489216]{0:T(1024)(128)(4,1)}), s8[294912]{0:T(1024)(128)(4,1)S(1)}, s32[]{:S(2)}) async-start(s8[4489216]{0:T(1024)(128)(4,1)} %bitcast.62), calls=%async_computation.5 | async-start | bytes 589824
  267.7 2.4 copy-start.1
  270.1 50.4 %collective-permute-start.2 = (bf16[16,137,4,128]{3,2,1,0:T(4,128)(2,1)S(1)}, bf16[16,137,4,128]{3,2,1,0:T(4,128)(2,1)S(1)}, u32[]{:S(2)}, u32[]{:S(2)}) collective-permute-start(bf16[16,137,4,128]{3,2,1,0:T(4,128)(2,1)S(1)} %get-tuple-element.6), channel_id=1, source_target_pairs={{8,0},{16,8},{24,16},{9,1},{17,9},{25,17},{10,2},{18,10},{26,18},{... | collective-permute-start | bytes 6733832 | tf_op jit(solution)/shard_map/ppermute | solution.py:15
  272.2 50.1 %collective-permute-start.3 = (bf16[16,137,4,128]{3,2,1,0:T(4,128)(2,1)S(1)}, bf16[16,137,4,128]{3,2,1,0:T(4,128)(2,1)S(1)}, u32[]{:S(2)}, u32[]{:S(2)}) collective-permute-start(bf16[16,137,4,128]{3,2,1,0:T(4,128)(2,1)S(1)} %get-tuple-element.7), channel_id=1, source_target_pairs={{0,8},{8,16},{16,24},{1,9},{9,17},{17,25},{2,10},{10,18},{18,26},{... | collective-permute-start | bytes 6733832 | tf_op jit(solution)/shard_map/ppermute | solution.py:12
where the time goes:
time: 484 us; the launch traced here: 482 us
  blocking collectives  166 us (34%)
  local copies, waits for them, and re-layouts  104 us (21%)
  waiting for transfers between devices  96 us (20%)
  other arithmetic  72.4 us (15%)
  matrix products  31 us (6%)
  starting transfers between devices  11 us (2%)
    all_to_all x1, blocking collectives, shards(): lax.all_to_all(spread_members, 'lon', split_axis=3, concat_axis=0, tiled=...  98.3 us
    all_to_all x1, blocking collectives, shards(): lax.all_to_all(spread_back, 'lon', split_axis=0, concat_axis=3, tiled=True)  56.5 us
    ppermute x2, waiting for transfers between devices, with_halo(): lax.ppermute(lax.slice_in_dim(block, block.shape[dim] - width, None, axis...  48.1 us
    ppermute x2, waiting for transfers between devices, with_halo(): lax.ppermute(lax.slice_in_dim(block, 0, width, axis=dim), axis, backward)  47.9 us
    reshape x2, local copies, waits for them, and re-layouts, shards(): spread_members = spread_members.astype(jnp.bfloat16).reshape(coarse.shape)  21.1 us
    reduce_sum x1, other arithmetic, shards(): increment = jnp.sum(ensemble.astype(jnp.float32) * stencil, axis=0)  20.3 us
    convert_element_type x1, other arithmetic, shards(): spread_back = spread_back.astype(jnp.bfloat16)  18 us
    add x1, other arithmetic, shards(): gradient = control + returned.astype(jnp.float32)  12.9 us
  transfers between devices with their start and end apart: 4, of which 4 were waited for; matrix products, arithmetic and copies ran while one was open for 0% of the time, Pallas kernels for 0%

commit v1 on v0

v1 whole, which is shorter than its diff:
```python
import functools

import jax
import jax.numpy as jnp
from jax import lax
from jax.experimental import pallas as pl
from jax.experimental.pallas import tpu as pltpu
from jax.sharding import PartitionSpec as P

F32, BF16 = jnp.float32, jnp.bfloat16
VMEM_LIMIT = 56 * 1024 * 1024


def lanes(block, width):
    return pl.ds(pl.multiple_of(block * width, width), width)


def vmem(count):
    return [pl.BlockSpec(memory_space=pltpu.VMEM)] * count


def vertical_block(fields, b, root, mixed, levels, height, width):
    pitch = mixed.shape[0] // height
    rows = jnp.concatenate(
        [fields[b, pl.ds(y, levels, stride=height), :] for y in range(height)], axis=1
    )
    out = jnp.dot(root[...], rows.astype(BF16), preferred_element_type=F32).astype(BF16)
    for y in range(height):
        mixed[y * pitch : y * pitch + levels, lanes(b, width)] = out[:, y * width : (y + 1) * width]


def longitude_block(b, blocks, bands, mixed, tile, levels, height, width):
    pitch = mixed.shape[0] // height
    parts = [mixed[:, lanes(lax.rem(b + blocks + o, blocks), width)] for o in (-1, 0, 1)]
    out = jnp.dot(jnp.concatenate(parts, axis=1), bands[b], preferred_element_type=F32)
    for y in range(height):
        tile[pl.ds(y, levels, stride=height), :] = out[y * pitch : y * pitch + levels]
    return tile[...].reshape(levels, height, width).astype(BF16)


def load_blocks(fields, k, held, sems, width, blocks):
    return [
        pltpu.make_async_copy(
            fields.at[k, :, pl.ds(b * width, width)], held.at[b], sems.at[b]
        )
        for b in range(blocks)
    ]


def forward_kernel(fields, root, bands, out, held, mixed, tile, sems, *, height, width):
    levels = root.shape[0]
    blocks = bands.shape[0]
    copies = load_blocks(fields, pl.program_id(0), held, sems, width, blocks)
    for copy in copies:
        copy.start()
    for b in range(blocks):
        copies[b].wait()
        vertical_block(held, b, root, mixed, levels, height, width)

    def longitude(b, _):
        out[b, 0] = longitude_block(b, blocks, bands, mixed, tile, levels, height, width)
        return 0

    lax.fori_loop(0, blocks, longitude, 0)


def row_index(width):
    return lax.broadcasted_iota(jnp.int32, (8, width), 0)


def forward_taps(taps, half, width):
    y = row_index(width)
    zero = jnp.zeros((8, width), F32)
    tap = lambda o: jnp.broadcast_to(taps[o + half : o + half + 1, :], (8, width))
    own, beyond = [tap(0)], [None]
    for r in range(1, 8):
        up = tap(r) if r <= half else zero
        down = tap(r - 8) if 8 - r <= half else zero
        own.append(jnp.where(y < 8 - r, up, down))
        beyond.append(jnp.where(y < 8 - r, down, up))
    return own, beyond


def stencil_level(spread, ensemble, beyond_ensemble, own_taps, beyond_taps):
    own = own_taps[0] * spread
    beyond = None
    for r in range(1, 8):
        turned = pltpu.roll(spread, 8 - r, 0)
        own = own + own_taps[r] * turned
        part = beyond_taps[r] * turned
        beyond = part if beyond is None else beyond + part
    return ensemble * own, beyond_ensemble * beyond


def stencil_kernel(spread, ensemble, edge, taps, up, down, own_sum, beyond_sum, *, half):
    members, levels, _, width = spread.shape
    own_taps, beyond_taps = forward_taps(taps, half, width)
    low = row_index(width) < 4

    def level(l, _):
        own = jnp.zeros((8, width), F32)
        beyond = jnp.zeros((8, width), F32)
        for k in range(members):
            a, b = stencil_level(
                spread[k, l].astype(F32),
                ensemble[k, l].astype(F32),
                edge[k, l].astype(F32),
                own_taps,
                beyond_taps,
            )
            own, beyond = own + a, beyond + b
        own_sum[l] = own
        beyond_sum[l] = beyond
        up[l] = jnp.where(low, beyond, own)
        down[l] = jnp.where(low, own, beyond)
        return 0

    lax.fori_loop(0, levels, level, 0)


def adjoint_level(own, beyond, taps, y):
    out = taps[0] * own
    for o, tap in taps.items():
        if o == 0:
            continue
        if o > 0:
            mixed = jnp.where(y < 8 - o, own, beyond)
        else:
            mixed = jnp.where(y >= -o, own, beyond)
        out = out + tap * pltpu.roll(mixed, o % 8, 0)
    return out


def adjoint_kernel(
    ensemble, edge, taps, own_sum, beyond_sum, below, above, innovation, inverse,
    edge_innovation, edge_inverse, departure, back, *, half
):
    members, levels, _, width = ensemble.shape
    y = row_index(width)
    low = y < 4
    tap = {
        o: jnp.broadcast_to(taps[o + half : o + half + 1, :], (8, width))
        for o in range(-half, half + 1)
    }

    def level(l, _):
        under, over = below[l], above[l]
        own = inverse[l] * (own_sum[l] + jnp.where(low, under, over) - innovation[l])
        beyond = edge_inverse[l] * (
            beyond_sum[l] + jnp.where(low, over, under) - edge_innovation[l]
        )
        departure[l] = own
        for k in range(members):
            a = (ensemble[k, l].astype(F32) * own).astype(BF16).astype(F32)
            b = (edge[k, l].astype(F32) * beyond).astype(BF16).astype(F32)
            back[k, l] = adjoint_level(a, b, tap, y).astype(BF16)
        return 0

    lax.fori_loop(0, levels, level, 0)


def adjoint_longitude(c, blocks, bands, flat, summed, width):
    before, after = lax.rem(c + blocks - 1, blocks), lax.rem(c + 1, blocks)
    left = jnp.concatenate([flat[:, lanes(b, width)] for b in (before, c, after)], axis=1)
    right = jnp.concatenate(
        [
            bands[before, 2 * width : 3 * width],
            bands[c, width : 2 * width],
            bands[after, 0:width],
        ],
        axis=1,
    )
    summed[c] = lax.dot_general(
        left, right, (((1,), (1,)), ((), ())), preferred_element_type=F32
    )


def adjoint_vertical(c, root, summed, held, levels, height, width):
    rows = [pl.ds(y, levels, stride=height) for y in range(height)]
    right = jnp.concatenate([summed[c, row, :] for row in rows], axis=1)
    out = lax.dot_general(
        root[...], right.astype(BF16), (((0,), (0,)), ((), ())), preferred_element_type=F32
    )
    out = out.astype(BF16).astype(F32)
    for y, row in enumerate(rows):
        held[c, row, :] = held[c, row, :] + out[:, y * width : (y + 1) * width]


def final_kernel(
    back, root, bands, control, gradient, held, flat, summed, in_sems, out_sems, *, height, width
):
    levels = root.shape[0]
    blocks = bands.shape[0]
    k = pl.program_id(0)
    copies = load_blocks(control, k, held, in_sems, width, blocks)
    for copy in copies:
        copy.start()

    def place(b, _):
        rows = back[b, 0].astype(F32).reshape(levels * height, width)
        flat[:, lanes(b, width)] = rows.astype(BF16)
        return 0

    lax.fori_loop(0, blocks, place, 0)

    def longitude(c, _):
        adjoint_longitude(c, blocks, bands, flat, summed, width)
        return 0

    lax.fori_loop(0, blocks, longitude, 0)
    stores = [
        pltpu.make_async_copy(
            held.at[b], gradient.at[k, :, pl.ds(b * width, width)], out_sems.at[b]
        )
        for b in range(blocks)
    ]
    for c in range(blocks):
        copies[c].wait()
        adjoint_vertical(c, root, summed, held, levels, height, width)
        stores[c].start()
    for store in stores:
        store.wait()


def shards(control, ensemble, vertical_root, sector_band, latitude_taps, innovation, inverse_error):
    half = latitude_taps.shape[0] // 2
    width = sector_band.shape[1]
    own, levels, height, total = control.shape
    members = ensemble.shape[0]
    blocks = total // width
    lats = lax.axis_size("lat")
    forward = [(i, i + 1) for i in range(lats - 1)]
    backward = [(i + 1, i) for i in range(lats - 1)]
    params = pltpu.CompilerParams(vmem_limit_bytes=VMEM_LIMIT)

    bands = lax.all_gather(sector_band, "lon", axis=0, tiled=False)
    bands = bands.reshape(blocks, 3 * width, width)

    def edges(array, dim):
        mid = height // 2
        low = lax.ppermute(lax.slice_in_dim(array, 0, mid, axis=dim), "lat", backward)
        high = lax.ppermute(lax.slice_in_dim(array, mid, height, axis=dim), "lat", forward)
        return jnp.concatenate([low, high], axis=dim)

    edge = edges(ensemble, 2)
    edge_innovation, edge_inverse = edges(innovation, 1), edges(inverse_error, 1)

    fields = control.reshape(own, levels * height, total)
    pitch = -(-levels // 16) * 16
    whole = lambda *shape: pl.BlockSpec(shape, lambda k: (0,) * len(shape))
    spread = pl.pallas_call(
        functools.partial(forward_kernel, height=height, width=width),
        grid=(own,),
        in_specs=[
            pl.BlockSpec(memory_space=pl.ANY),
            whole(levels, levels),
            whole(blocks, 3 * width, width),
        ],
        out_specs=pl.BlockSpec((blocks, 1, levels, height, width), lambda k: (0, k, 0, 0, 0)),
        out_shape=jax.ShapeDtypeStruct((blocks, own, levels, height, width), BF16),
        scratch_shapes=[
            pltpu.VMEM((blocks, levels * height, width), F32),
            pltpu.VMEM((height * pitch, total), BF16),
            pltpu.VMEM((levels * height, width), F32),
            pltpu.SemaphoreType.DMA((blocks,)),
        ],
        compiler_params=params,
        name="spread",
    )(fields, vertical_root, bands)
    spread = lax.all_to_all(spread, "lon", split_axis=0, concat_axis=0, tiled=True)
    spread = spread.reshape(members, levels, height, width)
    sums = jax.ShapeDtypeStruct((levels, height, width), F32)
    up, down, own_sum, beyond_sum = pl.pallas_call(
        functools.partial(stencil_kernel, half=half),
        in_specs=vmem(4),
        out_specs=vmem(4),
        out_shape=[sums] * 4,
        compiler_params=params,
        name="stencil",
    )(spread, ensemble, edge, latitude_taps)
    below = lax.ppermute(up, "lat", forward)
    above = lax.ppermute(down, "lat", backward)
    departure, back = pl.pallas_call(
        functools.partial(adjoint_kernel, half=half),
        in_specs=vmem(11),
        out_specs=vmem(2),
        out_shape=[sums, jax.ShapeDtypeStruct((members, levels, height, width), BF16)],
        compiler_params=params,
        name="adjoint",
    )(
        ensemble, edge, latitude_taps, own_sum, beyond_sum, below, above, innovation,
        inverse_error, edge_innovation, edge_inverse,
    )
    back = back.reshape(blocks, own, levels, height, width)
    back = lax.all_to_all(back, "lon", split_axis=0, concat_axis=0, tiled=True)
    gradient = pl.pallas_call(
        functools.partial(final_kernel, height=height, width=width),
        grid=(own,),
        in_specs=[
            pl.BlockSpec((blocks, 1, levels, height, width), lambda k: (0, k, 0, 0, 0)),
            whole(levels, levels),
            whole(blocks, 3 * width, width),
            pl.BlockSpec(memory_space=pl.ANY),
        ],
        out_specs=pl.BlockSpec(memory_space=pl.ANY),
        out_shape=jax.ShapeDtypeStruct((own, levels * height, total), F32),
        scratch_shapes=[
            pltpu.VMEM((blocks, levels * height, width), F32),
            pltpu.VMEM((levels * height, total), BF16),
            pltpu.VMEM((blocks, levels * height, width), F32),
            pltpu.SemaphoreType.DMA((blocks,)),
            pltpu.SemaphoreType.DMA((blocks,)),
        ],
        compiler_params=params,
        name="final",
    )(back, vertical_root, bands, fields)
    return gradient.reshape(control.shape), departure


def solution(mesh):
    placed = (
        P("lon", None, "lat", None),
        P(None, None, "lat", "lon"),
        P(),
        P(None, None, "lon"),
        P(None, "lon"),
        P(None, "lat", "lon"),
        P(None, "lat", "lon"),
    )
    return jax.shard_map(
        shards,
        mesh=mesh,
        in_specs=placed,
        out_specs=(P("lon", None, "lat", None), P(None, "lat", "lon")),
        check_vma=False,
    )
```

time: 484 us -> 246 us (0.51)
  local copies, waits for them, and re-layouts: 104 us -> 6.58 us
  blocking collectives: 166 us -> 71.1 us
  Pallas kernels: 0 us -> 77.3 us
  other arithmetic: 72.4 us -> 6.27 us
  waiting for transfers between devices: 96 us -> 53.9 us
  matrix products: 31 us -> 0 us
  starting transfers between devices: 11 us -> 27 us
    all_to_all x2 -> x1, blocking collectives: 155 us -> 59.2 us  [shards(): back = lax.all_to_all(back, 'lon', split_axis=0, concat_axis=0, tiled=True)]
    pallas_call x0 -> x4, Pallas kernels: none -> 77.3 us  [the longest x1 21.4 us: shards(): pl.pallas_call(functools.partial(stencil_kernel, half=half), in_specs=vme...]
    ppermute x4 -> x8, waiting for transfers between devices: 96 us -> 53.9 us  [the longest x3 52.2 us: edges(): lax.ppermute(lax.slice_in_dim(array, 0, mid, axis=dim), 'lat', backward)]
    convert_element_type x5 -> x0, other arithmetic: 39.1 us -> none  [the longest x1 18 us: shards(): spread_back = spread_back.astype(jnp.bfloat16)]
    convert_element_type x3 -> x0, local copies, waits for them, and re-layouts: 31.3 us -> none  [the longest x1 10.5 us: shards(): gradient = control + returned.astype(jnp.float32)]
    dot_general x4 -> x0, matrix products: 31 us -> none  [the longest x1 12 us: shards(): jnp.einsum('rbj,bkj->rbk', blocks_back, band_blocks, preferred_element_ty...]
    reshape x4 -> x0, local copies, waits for them, and re-layouts: 26.4 us -> none  [the longest x2 21.1 us: shards(): spread_members = spread_members.astype(jnp.bfloat16).reshape(coarse.shape)]
    reduce_sum x1 -> x0, other arithmetic: 20.3 us -> none  [shards(): increment = jnp.sum(ensemble.astype(jnp.float32) * stencil, axis=0)]
  transfers between devices with their start and end apart: 4 -> 9, of which waited for: 4 -> 3; matrix products, arithmetic and copies ran while one was open for 0% -> 5% of each run, Pallas kernels for 0% -> 9%
where the time goes in v1:
time: 246 us; the launch traced here: 243 us
  Pallas kernels  77.3 us (31%)
  blocking collectives  71.1 us (29%)
  waiting for transfers between devices  53.9 us (22%)
  starting transfers between devices  27 us (11%)
  local copies, waits for them, and re-layouts  6.58 us (3%)
  other arithmetic  6.27 us (3%)
    all_to_all x1, blocking collectives, shards(): back = lax.all_to_all(back, 'lon', split_axis=0, concat_axis=0, tiled=True)  59.2 us
    ppermute x3, waiting for transfers between devices, edges(): lax.ppermute(lax.slice_in_dim(array, 0, mid, axis=dim), 'lat', backward)  52.2 us
    pallas_call x1, Pallas kernels, shards(): pl.pallas_call(functools.partial(stencil_kernel, half=half), in_specs=vme...  21.4 us
    pallas_call x1, Pallas kernels, shards(): pl.pallas_call(functools.partial(adjoint_kernel, half=half), in_specs=vme...  21 us
    pallas_call x1, Pallas kernels, shards(): pl.pallas_call(functools.partial(final_kernel, height=height, width=width...  18 us
    pallas_call x1, Pallas kernels, shards(): pl.pallas_call(functools.partial(forward_kernel, height=height, width=wid...  16.9 us
    all_gather x1, blocking collectives, shards(): bands = lax.all_gather(sector_band, 'lon', axis=0, tiled=False)  11.9 us
    ppermute x3, starting transfers between devices, edges(): lax.ppermute(lax.slice_in_dim(array, mid, height, axis=dim), 'lat', forward)  9.92 us
  transfers between devices with their start and end apart: 9, of which 3 were waited for; matrix products, arithmetic and copies ran while one was open for 5% of the time, Pallas kernels for 9%

profile of v1, /device:TPU:19, one launch (start us, length us, event | category | flops | bytes accessed | tf_op | source)
XLA Modules:
  0.0 243.1 jit_solution(18115621249566658007)
XLA Ops:
  0.6 11.9 %all-gather = bf16[24,128,128]{2,1,0:T(8,128)(2,1)} all-gather(bf16[3,128,128]{2,1,0:T(8,128)(2,1)} %param.10), channel_id=2, replica_groups=mesh['lat'=4,'lon'=8] {'lon'}, dimensions={0}, use_global_device_ids=true | all-gather | bytes 884736 | tf_op jit(solution)/shard_map/all_gather | solution.py:236
  12.5 16.9 %spread.1 = bf16[8,2,137,8,128]{4,3,2,1,0:T(8,128)(2,1)} custom-call(f32[2,1096,1024]{2,1,0:T(8,128)} %bitcast.5, bf16[137,137]{1,0:T(8,128)(2,1)} %root.3, bf16[8,384,128]{2,1,0:T(8,128)(2,1)} %bitcast.8), custom_call_target="tpu_custom_call" | custom-call | tf_op jit(solution)/shard_map/spread/pallas_call | solution.py:251
  29.4 5.8 %all-to-all-start = ((bf16[8,2,137,8,128]{4,3,2,1,0:T(8,128)(2,1)}), bf16[8,2,137,8,128]{4,3,2,1,0:T(8,128)(2,1)}, u32[]{:S(2)}, u32[]{:S(2)}) async-start(bf16[8,2,137,8,128]{4,3,2,1,0:T(8,128)(2,1)} %spread.1), calls=%async_computation | async-start | bytes 8978432 | tf_op jit(solution)/shard_map/all_to_all | solution.py:270
  35.2 5.4 %fusion = (bf16[16,137,4,128]{3,2,1,0:T(4,128)(2,1)S(1)}, bf16[16,137,4,128]{3,2,1,0:T(4,128)(2,1)S(1)}) fusion(bf16[16,137,8,128]{3,2,1,0:T(8,128)(2,1)} %ensemble.3), kind=kLoop, calls=%fused_computation.3 | loop fusion | bytes 8978432 | tf_op jit(solution)/shard_map/slice | solution.py:241
  40.6 2.1 collective-permute-start
  42.7 3.4 %collective-permute-start.1 = (bf16[16,137,4,128]{3,2,1,0:T(4,128)(2,1)S(1)}, bf16[16,137,4,128]{3,2,1,0:T(4,128)(2,1)S(1)}, u32[]{:S(2)}, u32[]{:S(2)}) collective-permute-start(bf16[16,137,4,128]{3,2,1,0:T(4,128)(2,1)S(1)} %get-tuple-element.15), channel_id=1, source_target_pairs={{0,8},{8,16},{16,24},{1,9},{9,17},{17,25},{2,10},{10,18},{18,26},{... | collective-permute-start | bytes 6733832 | tf_op jit(solution)/shard_map/ppermute | solution.py:242
  46.0 0.1 fusion.2
  46.1 1.9 collective-permute-start.4
  48.1 3.4 %collective-permute-start.5 = (f32[137,4,128]{2,1,0:T(4,128)S(1)}, f32[137,4,128]{2,1,0:T(4,128)S(1)}, u32[]{:S(2)}, u32[]{:S(2)}) collective-permute-start(f32[137,4,128]{2,1,0:T(4,128)S(1)} %get-tuple-element.19), channel_id=1, source_target_pairs={{0,8},{8,16},{16,24},{1,9},{9,17},{17,25},{2,10},{10,18},{18,26},{... | collective-permute-start | bytes 841736 | tf_op jit(solution)/shard_map/ppermute | solution.py:242
  51.4 41.1 %collective-permute-done = bf16[16,137,4,128]{3,2,1,0:T(4,128)(2,1)S(1)} collective-permute-done((bf16[16,137,4,128]{3,2,1,0:T(4,128)(2,1)S(1)}, bf16[16,137,4,128]{3,2,1,0:T(4,128)(2,1)S(1)}, u32[]{:S(2)}, u32[]{:S(2)}) %collective-permute-start) | collective-permute-done | bytes 2244640 | tf_op jit(solution)/shard_map/ppermute | solution.py:241
  92.5 1.8 collective-permute-done.1
  94.2 4.4 %pad_maximum_fusion.edge = bf16[16,137,8,128]{3,2,1,0:T(8,128)(2,1)} fusion(bf16[16,137,4,128]{3,2,1,0:T(4,128)(2,1)S(1)} %collective-permute-done.1, bf16[16,137,4,128]{3,2,1,0:T(4,128)(2,1)S(1)} %collective-permute-done), kind=kLoop, calls=%fused_computation | loop fusion | flops 8978432 | bytes 8978432 | tf_op jit(solution)/shard_map/concatenate | solution.py:243
  98.7 0.0 all-to-all-done
  98.7 21.4 %stencil.1 = (f32[137,8,128]{2,1,0:T(8,128)}, f32[137,8,128]{2,1,0:T(8,128)}, f32[137,8,128]{2,1,0:T(8,128)}, f32[137,8,128]{2,1,0:T(8,128)}) custom-call(bf16[16,137,8,128]{3,2,1,0:T(8,128)(2,1)} %bitcast.2.spread, bf16[16,137,8,128]{3,2,1,0:T(8,128)(2,1)} %ensemble.3, bf16[16,137,8,128]{3,2,1,0:T(8,128)(2,1)} %pad_maximum_fusion.edge, f32[9,128]{1,0:T(8,128)} %taps.3), custom_call_target="tpu_custom_call" | custom-call | tf_op jit(solution)/shard_map/stencil/pallas_call | solution.py:273
  120.1 3.3 %collective-permute-start.2 = (f32[137,8,128]{2,1,0:T(8,128)}, f32[137,8,128]{2,1,0:T(8,128)S(1)}, u32[]{:S(2)}, u32[]{:S(2)}) collective-permute-start(f32[137,8,128]{2,1,0:T(8,128)} %get-tuple-element.10), channel_id=1, source_target_pairs={{0,8},{8,16},{16,24},{1,9},{9,17},{17,25},{2,10},{10,18},{18,26},{... | collective-permute-start | bytes 1683464 | tf_op jit(solution)/shard_map/ppermute | solution.py:281
  123.4 1.9 collective-permute-start.3
  125.4 0.1 fusion.1
  125.5 2.1 collective-permute-start.6
  127.6 0.0 collective-permute-done.4
  127.6 3.2 %collective-permute-start.7 = (f32[137,4,128]{2,1,0:T(4,128)S(1)}, f32[137,4,128]{2,1,0:T(4,128)S(1)}, u32[]{:S(2)}, u32[]{:S(2)}) collective-permute-start(f32[137,4,128]{2,1,0:T(4,128)S(1)} %get-tuple-element.17), channel_id=1, source_target_pairs={{0,8},{8,16},{16,24},{1,9},{9,17},{17,25},{2,10},{10,18},{18,26},{... | collective-permute-start | bytes 841736 | tf_op jit(solution)/shard_map/ppermute | solution.py:242
  130.8 0.0 collective-permute-done.5
  130.8 0.9 pad_maximum_fusion.1.edge_innovation
  131.7 11.1 %collective-permute-done.6 = f32[137,4,128]{2,1,0:T(4,128)S(1)} collective-permute-done((f32[137,4,128]{2,1,0:T(4,128)S(1)}, f32[137,4,128]{2,1,0:T(4,128)S(1)}, u32[]{:S(2)}, u32[]{:S(2)}) %collective-permute-start.6) | collective-permute-done | bytes 280608 | tf_op jit(solution)/shard_map/ppermute | solution.py:241
  142.9 0.0 collective-permute-done.7
  142.9 0.9 pad_maximum_fusion.2.edge_inverse
  143.8 0.0 collective-permute-done.2.below
  143.8 0.0 collective-permute-done.3.above
  143.8 0.8 copy-done.2
  144.6 0.2 copy-done.3
  144.8 21.0 %adjoint.1 = (f32[137,8,128]{2,1,0:T(8,128)}, bf16[16,137,8,128]{3,2,1,0:T(8,128)(2,1)}) custom-call(bf16[16,137,8,128]{3,2,1,0:T(8,128)(2,1)} %ensemble.3, bf16[16,137,8,128]{3,2,1,0:T(8,128)(2,1)} %pad_maximum_fusion.edge, f32[9,128]{1,0:T(8,128)} %taps.3, f32[137,8,128]{2,1,0:T(8,128)} %get-tuple-element.8.own_sum, ...), custom_call_target="tpu_custom_call" | custom-call | tf_op jit(solution)/shard_map/adjoint/pallas_call | solution.py:283
  165.8 59.2 %all_to_all.10.back = bf16[8,2,137,8,128]{4,3,2,1,0:T(8,128)(2,1)} all-to-all(bf16[8,2,137,8,128]{4,3,2,1,0:T(8,128)(2,1)} %bitcast.10), channel_id=1, replica_groups=mesh['lat'=4,'lon'=8] {'lon'}, dimensions={0} | all-to-all | bytes 8978432 | tf_op jit(solution)/shard_map/all_to_all | solution.py:295
  225.0 18.0 %final.1 = f32[2,1096,1024]{2,1,0:T(8,128)} custom-call(bf16[8,2,137,8,128]{4,3,2,1,0:T(8,128)(2,1)} %all_to_all.10.back, bf16[137,137]{1,0:T(8,128)(2,1)} %root.3, bf16[8,384,128]{2,1,0:T(8,128)(2,1)} %bitcast.9, f32[2,1096,1024]{2,1,0:T(8,128)} %bitcast.6), custom_call_target="tpu_custom_call" | custom-call | tf_op jit(solution)/shard_map/final/pallas_call | solution.py:296
  (6 shorter events, 0.0 us)
Async XLA Ops:
  29.4 69.3 %all-to-all-start = ((bf16[8,2,137,8,128]{4,3,2,1,0:T(8,128)(2,1)}), bf16[8,2,137,8,128]{4,3,2,1,0:T(8,128)(2,1)}, u32[]{:S(2)}, u32[]{:S(2)}) async-start(bf16[8,2,137,8,128]{4,3,2,1,0:T(8,128)(2,1)} %spread.1), calls=%async_computation | async-start | bytes 8978432 | tf_op jit(solution)/shard_map/all_to_all | solution.py:270
  35.2 10.9 %copy-start = (f32[137,8,128]{2,1,0:T(8,128)S(1)}, f32[137,8,128]{2,1,0:T(8,128)}, u32[]{:S(2)}) copy-start(f32[137,8,128]{2,1,0:T(8,128)} %innovation.1) | copy-start | bytes 1683460
  40.6 51.9 %collective-permute-start = (bf16[16,137,4,128]{3,2,1,0:T(4,128)(2,1)S(1)}, bf16[16,137,4,128]{3,2,1,0:T(4,128)(2,1)S(1)}, u32[]{:S(2)}, u32[]{:S(2)}) collective-permute-start(bf16[16,137,4,128]{3,2,1,0:T(4,128)(2,1)S(1)} %get-tuple-element.14), channel_id=1, source_target_pairs={{8,0},{16,8},{24,16},{9,1},{17,9},{25,17},{10,2},{18,10},{26,18},{... | collective-permute-start | bytes 6733832 | tf_op jit(solution)/shard_map/ppermute | solution.py:241
  42.7 51.6 %collective-permute-start.1 = (bf16[16,137,4,128]{3,2,1,0:T(4,128)(2,1)S(1)}, bf16[16,137,4,128]{3,2,1,0:T(4,128)(2,1)S(1)}, u32[]{:S(2)}, u32[]{:S(2)}) collective-permute-start(bf16[16,137,4,128]{3,2,1,0:T(4,128)(2,1)S(1)} %get-tuple-element.15), channel_id=1, source_target_pairs={{0,8},{8,16},{16,24},{1,9},{9,17},{17,25},{2,10},{10,18},{18,26},{... | collective-permute-start | bytes 6733832 | tf_op jit(solution)/shard_map/ppermute | solution.py:242
  46.1 81.5 %collective-permute-start.4 = (f32[137,4,128]{2,1,0:T(4,128)S(1)}, f32[137,4,128]{2,1,0:T(4,128)S(1)}, u32[]{:S(2)}, u32[]{:S(2)}) collective-permute-start(f32[137,4,128]{2,1,0:T(4,128)S(1)} %get-tuple-element.18), channel_id=1, source_target_pairs={{8,0},{16,8},{24,16},{9,1},{17,9},{25,17},{10,2},{18,10},{26,18},{... | collective-permute-start | bytes 841736 | tf_op jit(solution)/shard_map/ppermute | solution.py:241
  48.1 82.8 %collective-permute-start.5 = (f32[137,4,128]{2,1,0:T(4,128)S(1)}, f32[137,4,128]{2,1,0:T(4,128)S(1)}, u32[]{:S(2)}, u32[]{:S(2)}) collective-permute-start(f32[137,4,128]{2,1,0:T(4,128)S(1)} %get-tuple-element.19), channel_id=1, source_target_pairs={{0,8},{8,16},{16,24},{1,9},{9,17},{17,25},{2,10},{10,18},{18,26},{... | collective-permute-start | bytes 841736 | tf_op jit(solution)/shard_map/ppermute | solution.py:242
  98.7 26.7 %copy-start.1 = (f32[137,8,128]{2,1,0:T(8,128)S(1)}, f32[137,8,128]{2,1,0:T(8,128)}, u32[]{:S(2)}) copy-start(f32[137,8,128]{2,1,0:T(8,128)} %inverse.1) | copy-start | bytes 1683460
  120.1 23.7 %collective-permute-start.2 = (f32[137,8,128]{2,1,0:T(8,128)}, f32[137,8,128]{2,1,0:T(8,128)S(1)}, u32[]{:S(2)}, u32[]{:S(2)}) collective-permute-start(f32[137,8,128]{2,1,0:T(8,128)} %get-tuple-element.10), channel_id=1, source_target_pairs={{0,8},{8,16},{16,24},{1,9},{9,17},{17,25},{2,10},{10,18},{18,26},{... | collective-permute-start | bytes 1683464 | tf_op jit(solution)/shard_map/ppermute | solution.py:281
  123.4 20.4 %collective-permute-start.3 = (f32[137,8,128]{2,1,0:T(8,128)}, f32[137,8,128]{2,1,0:T(8,128)S(1)}, u32[]{:S(2)}, u32[]{:S(2)}) collective-permute-start(f32[137,8,128]{2,1,0:T(8,128)} %get-tuple-element.11), channel_id=1, source_target_pairs={{8,0},{16,8},{24,16},{9,1},{17,9},{25,17},{10,2},{18,10},{26,18},{... | collective-permute-start | bytes 1683464 | tf_op jit(solution)/shard_map/ppermute | solution.py:282
  125.5 17.4 %collective-permute-start.6 = (f32[137,4,128]{2,1,0:T(4,128)S(1)}, f32[137,4,128]{2,1,0:T(4,128)S(1)}, u32[]{:S(2)}, u32[]{:S(2)}) collective-permute-start(f32[137,4,128]{2,1,0:T(4,128)S(1)} %get-tuple-element.16), channel_id=1, source_target_pairs={{8,0},{16,8},{24,16},{9,1},{17,9},{25,17},{10,2},{18,10},{26,18},{... | collective-permute-start | bytes 841736 | tf_op jit(solution)/shard_map/ppermute | solution.py:241
  127.6 15.3 %collective-permute-start.7 = (f32[137,4,128]{2,1,0:T(4,128)S(1)}, f32[137,4,128]{2,1,0:T(4,128)S(1)}, u32[]{:S(2)}, u32[]{:S(2)}) collective-permute-start(f32[137,4,128]{2,1,0:T(4,128)S(1)} %get-tuple-element.17), channel_id=1, source_target_pairs={{0,8},{8,16},{16,24},{1,9},{9,17},{17,25},{2,10},{10,18},{18,26},{... | collective-permute-start | bytes 841736 | tf_op jit(solution)/shard_map/ppermute | solution.py:242
  143.8 0.8 copy-start.2
  143.8 1.0 copy-start.3

commit v2 on v0

v2 whole, which is shorter than its diff:
```python
import functools

import jax
import jax.numpy as jnp
from jax import lax
from jax.experimental import pallas as pl
from jax.experimental.pallas import tpu as pltpu
from jax.sharding import PartitionSpec as P

F32, BF16 = jnp.float32, jnp.bfloat16
VMEM_LIMIT = 62 * 1024 * 1024


def lanes(block, width):
    return pl.ds(pl.multiple_of(block * width, width), width)


def vertical_block(fields, b, root, mixed, levels, height, width):
    pitch = mixed.shape[0] // height
    rows = jnp.concatenate(
        [fields[b, pl.ds(y, levels, stride=height), :] for y in range(height)], axis=1
    )
    out = jnp.dot(root[...], rows.astype(BF16), preferred_element_type=F32).astype(BF16)
    for y in range(height):
        mixed[y * pitch : y * pitch + levels, lanes(b, width)] = out[:, y * width : (y + 1) * width]


def longitude_block(b, blocks, bands, mixed, tile, levels, height, width):
    pitch = mixed.shape[0] // height
    parts = [mixed[:, lanes(lax.rem(b + blocks + o, blocks), width)] for o in (-1, 0, 1)]
    out = jnp.dot(jnp.concatenate(parts, axis=1), bands[b], preferred_element_type=F32)
    for y in range(height):
        tile[pl.ds(y, levels, stride=height), :] = out[y * pitch : y * pitch + levels]
    return tile[...].reshape(levels, height, width).astype(BF16)


def row_index(width):
    return lax.broadcasted_iota(jnp.int32, (8, width), 0)


def forward_taps(taps, half, width):
    y = row_index(width)
    zero = jnp.zeros((8, width), F32)
    tap = lambda o: jnp.broadcast_to(taps[o + half : o + half + 1, :], (8, width))
    own, beyond = [tap(0)], [None]
    for r in range(1, 8):
        up = tap(r) if r <= half else zero
        down = tap(r - 8) if 8 - r <= half else zero
        own.append(jnp.where(y < 8 - r, up, down))
        beyond.append(jnp.where(y < 8 - r, down, up))
    return own, beyond


def stencil_level(spread, ensemble, beyond_ensemble, own_taps, beyond_taps):
    own = own_taps[0] * spread
    beyond = None
    for r in range(1, 8):
        turned = pltpu.roll(spread, 8 - r, 0)
        own = own + own_taps[r] * turned
        part = beyond_taps[r] * turned
        beyond = part if beyond is None else beyond + part
    return ensemble * own, beyond_ensemble * beyond


def adjoint_level(own, beyond, taps, y):
    out = taps[0] * own
    for o, tap in taps.items():
        if o == 0:
            continue
        if o > 0:
            mixed = jnp.where(y < 8 - o, own, beyond)
        else:
            mixed = jnp.where(y >= -o, own, beyond)
        out = out + tap * pltpu.roll(mixed, o % 8, 0)
    return out


def adjoint_longitude(c, blocks, bands, flat, summed, width):
    before, after = lax.rem(c + blocks - 1, blocks), lax.rem(c + 1, blocks)
    left = jnp.concatenate([flat[:, lanes(b, width)] for b in (before, c, after)], axis=1)
    right = jnp.concatenate(
        [
            bands[before, 2 * width : 3 * width],
            bands[c, width : 2 * width],
            bands[after, 0:width],
        ],
        axis=1,
    )
    summed[c] = lax.dot_general(
        left, right, (((1,), (1,)), ((), ())), preferred_element_type=F32
    )


def adjoint_vertical(c, root, summed, held, levels, height, width):
    rows = [pl.ds(y, levels, stride=height) for y in range(height)]
    right = jnp.concatenate([summed[c, row, :] for row in rows], axis=1)
    out = lax.dot_general(
        root[...], right.astype(BF16), (((0,), (0,)), ((), ())), preferred_element_type=F32
    )
    out = out.astype(BF16).astype(F32)
    for y, row in enumerate(rows):
        held[c, row, :] = held[c, row, :] + out[:, y * width : (y + 1) * width]


def program(
    fields, ensemble, root, band, taps, innovation, inverse, gradient, departure,
    held, mixed, tile, bands, send, spread, back, flat, summed,
    up, down, below, above, fact_up, fact_down, fact_below, fact_above,
    sum_up, sum_down, sum_below, sum_above, own_sum, beyond_sum,
    load_sem, store_sem, band_sems, spread_sems, back_sems, up_sems, down_sems,
    fact_sems, sum_sems, *, half
):
    members, levels, height, width = ensemble.shape
    own = fields.shape[0]
    blocks = bands.shape[0]
    me, row = lax.axis_index("lon"), lax.axis_index("lat")
    has_below, has_above = row > 0, row < lax.axis_size("lat") - 1
    mid = levels // 2
    y = row_index(width)
    low = y < 4

    def remote(source, target, sems, index, **device):
        return pltpu.make_async_remote_copy(
            src_ref=source, dst_ref=target,
            send_sem=sems.at[(0,) + index], recv_sem=sems.at[(1,) + index],
            device_id=device, device_id_type=pl.DeviceIdType.MESH,
        )

    def loop(start, stop, body, unroll=1):
        def step(i, _):
            body(i)
            return 0

        lax.fori_loop(start, stop, step, 0, unroll=unroll)

    def load(k, b):
        return pltpu.make_async_copy(
            fields.at[k, :, lanes(b, width)], held.at[k, b], load_sem.at[k, b]
        )

    def store(k, b):
        return pltpu.make_async_copy(
            held.at[k, b], gradient.at[k, :, lanes(b, width)], store_sem.at[k, b]
        )

    def to_above(source, target, sems, index):
        return remote(source, target, sems, index, lat=row + 1)

    def to_below(source, target, sems, index):
        return remote(source, target, sems, index, lat=row - 1)

    def both(action, pairs):
        for guard, copy in pairs:
            @pl.when(guard)
            def _():
                action(copy())

    for k in range(own):
        loop(0, blocks, lambda b: load(k, b).start())
    barrier = pltpu.get_barrier_semaphore()
    loop(1, blocks, lambda t: pl.semaphore_signal(
        barrier, inc=1, device_id={"lon": lax.rem(me + t, blocks)},
        device_id_type=pl.DeviceIdType.MESH))

    @pl.when(has_below)
    def _():
        pl.semaphore_signal(barrier, inc=1, device_id={"lat": row - 1},
                            device_id_type=pl.DeviceIdType.MESH)

    @pl.when(has_above)
    def _():
        pl.semaphore_signal(barrier, inc=1, device_id={"lat": row + 1},
                            device_id_type=pl.DeviceIdType.MESH)

    inner = jnp.logical_and(has_below, has_above)

    @pl.when(inner)
    def _():
        pl.semaphore_wait(barrier, blocks + 1)

    @pl.when(jnp.logical_not(inner))
    def _():
        pl.semaphore_wait(barrier, blocks)

    def band_send(t):
        target = lax.rem(me + t, blocks)
        pltpu.make_async_remote_copy(
            src_ref=band, dst_ref=bands.at[me], send_sem=band_sems.at[0, target],
            recv_sem=band_sems.at[1, me], device_id={"lon": target},
            device_id_type=pl.DeviceIdType.MESH,
        ).start()

    def band_wait(source):
        return pltpu.make_async_remote_copy(
            src_ref=band, dst_ref=bands.at[source], send_sem=band_sems.at[0, source],
            recv_sem=band_sems.at[1, source], device_id={"lon": source},
            device_id_type=pl.DeviceIdType.MESH,
        )

    loop(1, blocks, band_send)
    bands[me] = band[...]

    tiles = levels - mid

    def fold(a, b):
        return jnp.where(low, pltpu.roll(b, 4, 0), a), jnp.where(low, a, pltpu.roll(b, 4, 0))

    def unfold(under, over):
        return (
            jnp.where(low, over, under),
            pltpu.roll(jnp.where(low, under, over), 4, 0),
        )

    def edge_copies(k):
        return (
            (has_above, lambda: to_above(up.at[k], below.at[k], up_sems, (k,))),
            (has_below, lambda: to_below(down.at[k], above.at[k], down_sems, (k,))),
        )

    def edge_arrivals(k):
        return (
            (has_below, lambda: to_below(up.at[k], below.at[k], up_sems, (k,))),
            (has_above, lambda: to_above(down.at[k], above.at[k], down_sems, (k,))),
        )

    def edge_member(t, k):
        member = lax.rem(me + blocks - t, blocks) * own + k

        def pack(l):
            a, b = ensemble[member, l].astype(F32), ensemble[member, l + mid].astype(F32)
            high, bottom = fold(a, b)
            up[member, l] = high.astype(BF16)
            down[member, l] = bottom.astype(BF16)

        loop(0, tiles, pack)
        both(lambda copy: copy.start(), edge_copies(member))

    for k in range(own):
        loop(0, blocks, lambda t: edge_member(t, k))

    fact_copies = (
        (has_above, lambda: to_above(fact_up, fact_below, fact_sems, (0,))),
        (has_below, lambda: to_below(fact_down, fact_above, fact_sems, (1,))),
    )
    fact_arrivals = (
        (has_below, lambda: to_below(fact_up, fact_below, fact_sems, (0,))),
        (has_above, lambda: to_above(fact_down, fact_above, fact_sems, (1,))),
    )

    def pack_facts(l):
        fact_up[l], fact_down[l] = fold(innovation[l], inverse[l])

    loop(0, levels, pack_facts)
    both(lambda copy: copy.start(), fact_copies)

    @pl.when(row == 0)
    def _():
        def clear(k):
            below[k] = jnp.zeros(below.shape[1:], BF16)

        loop(0, members, clear)
        fact_below[...] = jnp.zeros(fact_below.shape, F32)
        sum_below[...] = jnp.zeros(sum_below.shape, F32)

    @pl.when(row == lax.axis_size("lat") - 1)
    def _():
        def clear(k):
            above[k] = jnp.zeros(above.shape[1:], BF16)

        loop(0, members, clear)
        fact_above[...] = jnp.zeros(fact_above.shape, F32)
        sum_above[...] = jnp.zeros(sum_above.shape, F32)

    def exchange(source, target, sems, k, peer):
        return pltpu.make_async_remote_copy(
            src_ref=source.at[peer, k], dst_ref=target.at[me, k],
            send_sem=sems.at[0, k, peer], recv_sem=sems.at[1, k, me],
            device_id={"lon": peer}, device_id_type=pl.DeviceIdType.MESH,
        )

    def arrival(source, target, sems, k, peer):
        return pltpu.make_async_remote_copy(
            src_ref=source.at[peer, k], dst_ref=target.at[peer, k],
            send_sem=sems.at[0, k, peer], recv_sem=sems.at[1, k, peer],
            device_id={"lon": peer}, device_id_type=pl.DeviceIdType.MESH,
        )

    for k in range(own):
        def vertical(b):
            load(k, b).wait()
            vertical_block(held.at[k], b, root, mixed, levels, height, width)

        loop(0, blocks, vertical)
        if k == 0:
            loop(1, blocks, lambda t: band_wait(lax.rem(me + t, blocks)).wait_recv())

        def longitude(t):
            b = lax.rem(me + t, blocks)
            value = longitude_block(b, blocks, bands, mixed, tile, levels, height, width)

            @pl.when(t < blocks)
            def _():
                send[b, k] = value
                exchange(send, spread, spread_sems, k, b).start()

            @pl.when(t == blocks)
            def _():
                spread[b, k] = value

        loop(1, blocks + 1, longitude)

    own_taps, beyond_taps = forward_taps(taps, half, width)

    def clear_sums(l):
        own_sum[l] = jnp.zeros((8, width), F32)
        beyond_sum[l] = jnp.zeros((8, width), F32)

    loop(0, levels, clear_sums)

    def stencil(t, k):
        source = lax.rem(me + blocks - t, blocks)
        member = source * own + k

        @pl.when(t > 0)
        def _():
            arrival(send, spread, spread_sems, k, source).wait_recv()

        both(lambda copy: copy.wait_recv(), edge_arrivals(member))

        def add(l, beyond_ensemble):
            a, b = stencil_level(
                spread[source, k, l].astype(F32), ensemble[member, l].astype(F32),
                beyond_ensemble, own_taps, beyond_taps,
            )
            own_sum[l] += a
            beyond_sum[l] += b

        def two(l):
            first, second = unfold(below[member, l].astype(F32), above[member, l].astype(F32))
            add(l, first)
            add(l + mid, second)

        loop(0, mid, two, 2 if mid % 2 == 0 else 1)
        if levels % 2:
            _, second = unfold(below[member, mid].astype(F32), above[member, mid].astype(F32))
            add(levels - 1, second)

    for k in range(own):
        loop(0, blocks, lambda t: stencil(t, k))

    def boundary(l):
        own_part, beyond_part = own_sum[l], beyond_sum[l]
        sum_up[l] = jnp.where(low, beyond_part, own_part)
        sum_down[l] = jnp.where(low, own_part, beyond_part)

    loop(0, levels, boundary)
    sum_copies = (
        (has_above, lambda: to_above(sum_up, sum_below, sum_sems, (0,))),
        (has_below, lambda: to_below(sum_down, sum_above, sum_sems, (1,))),
    )
    sum_arrivals = (
        (has_below, lambda: to_below(sum_up, sum_below, sum_sems, (0,))),
        (has_above, lambda: to_above(sum_down, sum_above, sum_sems, (1,))),
    )
    both(lambda copy: copy.start(), sum_copies)
    both(lambda copy: copy.wait_recv(), fact_arrivals)
    both(lambda copy: copy.wait_recv(), sum_arrivals)

    def depart(l):
        under, over = sum_below[l], sum_above[l]
        edge_innovation, edge_inverse = unfold(fact_below[l], fact_above[l])
        value = inverse[l] * (own_sum[l] + jnp.where(low, under, over) - innovation[l])
        departure[l] = value
        own_sum[l] = value
        beyond_sum[l] = edge_inverse * (
            beyond_sum[l] + jnp.where(low, over, under) - edge_innovation
        )

    loop(0, levels, depart)

    tap = {
        o: jnp.broadcast_to(taps[o + half : o + half + 1, :], (8, width))
        for o in range(-half, half + 1)
    }

    def adjoint(t, k):
        target = lax.rem(me + t, blocks)
        member = target * own + k

        def write(l, beyond_ensemble):
            a = (ensemble[member, l].astype(F32) * own_sum[l]).astype(BF16).astype(F32)
            b = (beyond_ensemble * beyond_sum[l]).astype(BF16).astype(F32)
            spread[target, k, l] = adjoint_level(a, b, tap, y).astype(BF16)

        def two(l):
            first, second = unfold(below[member, l].astype(F32), above[member, l].astype(F32))
            write(l, first)
            write(l + mid, second)

        loop(0, mid, two, 2 if mid % 2 == 0 else 1)
        if levels % 2:
            _, second = unfold(below[member, mid].astype(F32), above[member, mid].astype(F32))
            write(levels - 1, second)

        @pl.when(t < blocks)
        def _():
            exchange(spread, back, back_sems, k, target).start()

    for k in range(own):
        loop(1, blocks + 1, lambda t: adjoint(t, k))

    for k in range(own):
        def place(t):
            source = lax.rem(me + blocks - t, blocks)

            def put(value):
                rows = value.astype(F32).reshape(levels * height, width)
                flat[:, lanes(source, width)] = rows.astype(BF16)

            @pl.when(t == 0)
            def _():
                put(spread[source, k])

            @pl.when(t > 0)
            def _():
                arrival(spread, back, back_sems, k, source).wait_recv()
                put(back[source, k])

        loop(0, blocks, place)
        loop(0, blocks, lambda c: adjoint_longitude(c, blocks, bands, flat, summed, width))

        def finish(c):
            adjoint_vertical(c, root, summed, held.at[k], levels, height, width)
            store(k, c).start()

        loop(0, blocks, finish)

    for k in range(own):
        loop(0, blocks, lambda b: store(k, b).wait())

        def sent(t):
            peer = lax.rem(me + t, blocks)
            exchange(send, spread, spread_sems, k, peer).wait_send()
            exchange(spread, back, back_sems, k, peer).wait_send()

        loop(1, blocks, sent)
    loop(1, blocks, lambda t: band_wait(lax.rem(me + t, blocks)).wait_send())
    loop(0, members, lambda k: both(lambda copy: copy.wait_send(), edge_copies(k)))
    both(lambda copy: copy.wait_send(), fact_copies)
    both(lambda copy: copy.wait_send(), sum_copies)


def shards(control, ensemble, vertical_root, sector_band, latitude_taps, innovation, inverse_error):
    half = latitude_taps.shape[0] // 2
    width = sector_band.shape[1]
    own, levels, height, total = control.shape
    members = ensemble.shape[0]
    blocks = total // width
    pitch = -(-levels // 16) * 16
    tiles = levels - levels // 2
    rows = levels * height
    fields = control.reshape(own, rows, total)
    band = sector_band.reshape(3 * width, width)
    sums = (levels, height, width)
    dma = pltpu.SemaphoreType.DMA
    local = pl.BlockSpec(memory_space=pltpu.VMEM)
    remote = pl.BlockSpec(memory_space=pl.ANY)
    gradient, departure = pl.pallas_call(
        functools.partial(program, half=half),
        in_specs=[remote] + [local] * 6,
        out_specs=[remote, local],
        out_shape=[
            jax.ShapeDtypeStruct((own, rows, total), F32),
            jax.ShapeDtypeStruct(sums, F32),
        ],
        scratch_shapes=[
            pltpu.VMEM((own, blocks, rows, width), F32),
            pltpu.VMEM((height * pitch, total), BF16),
            pltpu.VMEM((rows, width), F32),
            pltpu.VMEM((blocks, 3 * width, width), BF16),
            pltpu.VMEM((blocks, own) + sums, BF16),
            pltpu.VMEM((blocks, own) + sums, BF16),
            pltpu.VMEM((blocks, own) + sums, BF16),
            pltpu.VMEM((rows, total), BF16),
            pltpu.VMEM((blocks, rows, width), F32),
        ]
        + [pltpu.VMEM((members, tiles, height, width), BF16)] * 4
        + [pltpu.VMEM(sums, F32)] * 10
        + [
            dma((own, blocks)),
            dma((own, blocks)),
            dma((2, blocks)),
            dma((2, own, blocks)),
            dma((2, own, blocks)),
            dma((2, members)),
            dma((2, members)),
            dma((2, 2)),
            dma((2, 2)),
        ],
        compiler_params=pltpu.CompilerParams(
            vmem_limit_bytes=VMEM_LIMIT, collective_id=0, has_side_effects=True
        ),
        name="gradient",
    )(fields, ensemble, vertical_root, band, latitude_taps, innovation, inverse_error)
    return gradient.reshape(control.shape), departure


def solution(mesh):
    placed = (
        P("lon", None, "lat", None),
        P(None, None, "lat", "lon"),
        P(),
        P(None, None, "lon"),
        P(None, "lon"),
        P(None, "lat", "lon"),
        P(None, "lat", "lon"),
    )
    return jax.shard_map(
        shards,
        mesh=mesh,
        in_specs=placed,
        out_specs=(P("lon", None, "lat", None), P(None, "lat", "lon")),
        check_vma=False,
    )
```

time: 484 us -> 157 us (0.32)
  blocking collectives: 166 us -> 0 us
  Pallas kernels: 0 us -> 147 us
  waiting for transfers between devices: 96 us -> 0 us
  local copies, waits for them, and re-layouts: 104 us -> 9.82 us
  other arithmetic: 72.4 us -> 0 us
  matrix products: 31 us -> 0 us
  starting transfers between devices: 11 us -> 0 us
    all_to_all x2 -> x0, blocking collectives: 155 us -> none  [the longest x1 98.3 us: shards(): lax.all_to_all(spread_members, 'lon', split_axis=3, concat_axis=0, tiled=...]
    pallas_call x0 -> x1, Pallas kernels: none -> 147 us  [shards(): pl.pallas_call(functools.partial(program, half=half), in_specs=[remote] +...]
    ppermute x4 -> x0, waiting for transfers between devices: 96 us -> none  [the longest x2 48.1 us: with_halo(): lax.ppermute(lax.slice_in_dim(block, block.shape[dim] - width, None, axis...]
    convert_element_type x5 -> x0, other arithmetic: 39.1 us -> none  [the longest x1 18 us: shards(): spread_back = spread_back.astype(jnp.bfloat16)]
    convert_element_type x3 -> x0, local copies, waits for them, and re-layouts: 31.3 us -> none  [the longest x1 10.5 us: shards(): gradient = control + returned.astype(jnp.float32)]
    dot_general x4 -> x0, matrix products: 31 us -> none  [the longest x1 12 us: shards(): jnp.einsum('rbj,bkj->rbk', blocks_back, band_blocks, preferred_element_ty...]
    reshape x4 -> x0, local copies, waits for them, and re-layouts: 26.4 us -> none  [the longest x2 21.1 us: shards(): spread_members = spread_members.astype(jnp.bfloat16).reshape(coarse.shape)]
    slice x6 -> x0, local copies, waits for them, and re-layouts: 20.8 us -> none  [the longest x2 12.7 us: shards(): jnp.roll(terms[..., :width], -1, axis=1)]
  transfers between devices with their start and end apart: 4 -> 0, of which waited for: 4 -> 0; matrix products, arithmetic and copies ran while one was open for 0% -> 0% of each run, Pallas kernels for 0% -> 0%
where the time goes in v2:
time: 157 us
  Pallas kernels  147 us (94%)
  local copies, waits for them, and re-layouts  9.82 us (6%)
    pallas_call x1, Pallas kernels, shards(): pl.pallas_call(functools.partial(program, half=half), in_specs=[remote] +...  147 us
    unnamed x4, local copies, waits for them, and re-layouts  9.82 us

profile of v2, /device:TPU:19, one launch (start us, length us, event | category | flops | bytes accessed | tf_op | source)
XLA Modules:
  0.0 157.1 jit_solution(59618237921283426)
XLA Ops:
  0.6 146.6 %gradient.1 = (f32[2,1096,1024]{2,1,0:T(8,128)}, f32[137,8,128]{2,1,0:T(8,128)}) custom-call(f32[2,1096,1024]{2,1,0:T(8,128)} %bitcast.4, bf16[16,137,8,128]{3,2,1,0:T(8,128)(2,1)} %ensemble.1, bf16[137,137]{1,0:T(8,128)(2,1)} %root.1, bf16[384,128]{1,0:T(8,128)(2,1)} %bitcast.5, f32[9,128]{1,0:T(8,128)} %taps.1, f32[137,8,128]{2,1,0:T(8,128)} %innovation.1, ...), custom_call_target="tpu_custom_call" | custom-call | tf_op jit(solution)/shard_map/gradient/pallas_call | solution.py:468
  147.2 0.0 copy-start
  147.2 9.0 %copy.11 = f32[2,137,8,1024]{3,2,1,0:T(8,128)} copy(f32[2,137,8,1024]{3,2,1,0:T(8,128)} %bitcast.3) | data formatting | bytes 17956864
  156.3 0.0 copy-done
  156.3 0.8 copy.12
Async XLA Ops:
  147.2 9.0 %copy-start = (f32[137,8,128]{2,1,0:T(8,128)S(1)}, f32[137,8,128]{2,1,0:T(8,128)}, u32[]{:S(2)}) copy-start(f32[137,8,128]{2,1,0:T(8,128)} %get-tuple-element.9) | copy-start | bytes 1683460
